TPU v7x, 32 devices: a whole 2x2x4 slice. The times are simulated.
32 devices in a mesh: dp: 4 (over y, x), expert: 8 (over z, core).
Axes of the slice: x: 2, y: 2, z: 4, core: 2. Of those that a mesh axis runs over, the one named last changes fastest.
Arguments:
- tokens: bfloat16 [1024, 1024], P(('dp', 'expert')), may hold values from -6 to 6
- cotangent: bfloat16 [1024, 1024], P(('dp', 'expert')), may hold values from -3 to 3
- routes: int32 [1024, 8], P(('dp', 'expert')), may hold values from 0 to 7, as said below
- combine: bfloat16 [1024, 8], P(('dp', 'expert')), may hold values from 0.099609375 to 1
- hot_experts: int32 [4], replicated, may hold values from 0 to 3, as said below
- extra_slots: int32 [4], replicated, may hold values from 1 to 4, as said below
- w_gate: bfloat16 [8, 1024, 384], P('expert'), may hold values from -0.1875 to 0.1875
- w_up: bfloat16 [8, 1024, 384], P('expert'), may hold values from -0.1875 to 0.1875
- w_down: bfloat16 [8, 384, 1024], P('expert'), may hold values from -0.3125 to 0.3125
Outputs:
- token_grads: bfloat16 [1024, 1024], P(('dp', 'expert'))
- grad_gate: bfloat16 [8, 1024, 384], P('expert', 'dp')
- grad_up: bfloat16 [8, 1024, 384], P('expert', 'dp')
- grad_down: bfloat16 [8, 384, 1024], P('expert')
Inputs may be any that keep to these rules, and one draw needn't show every extreme that they name: `routes`: each row names 8 different experts. `hot_experts`: 4 different experts, all below 4. `extra_slots`: one of the entries equals 4.
All inputs are finite; a program needn't handle non-finite values.
Results may differ from a plain program's by a relative error of at most 0.0064.
Values may be sent and summed in bfloat16 or wider, within the bound.
A program may use at most 64 MiB of HBM per device.

v0:
```python
import jax
import jax.numpy as jnp
from jax import lax
from jax.sharding import PartitionSpec as P


def forward_rows(weight_gate, weight_up, weight_down, row_tokens, row_cotan, row_weights):
    gate_pre = jnp.dot(row_tokens, weight_gate, preferred_element_type=jnp.float32)
    up_proj = jnp.dot(row_tokens, weight_up, preferred_element_type=jnp.float32)
    sigmoid_gate = jax.nn.sigmoid(gate_pre)
    gate_act = gate_pre * sigmoid_gate
    hidden = (gate_act * up_proj).astype(jnp.bfloat16)
    out_grad = (row_weights.astype(jnp.float32)[:, None] * row_cotan.astype(jnp.float32)).astype(
        jnp.bfloat16
    )
    hidden_grad = jnp.dot(out_grad, weight_down.T, preferred_element_type=jnp.float32)
    gate_grad = (
        hidden_grad * up_proj * sigmoid_gate * (1.0 + gate_pre * (1.0 - sigmoid_gate))
    ).astype(jnp.bfloat16)
    up_grad = (hidden_grad * gate_act).astype(jnp.bfloat16)
    row_grads = jnp.dot(gate_grad, weight_gate.T, preferred_element_type=jnp.float32)
    row_grads = row_grads + jnp.dot(up_grad, weight_up.T, preferred_element_type=jnp.float32)
    return (row_grads.astype(jnp.bfloat16), (row_tokens, gate_grad, up_grad, hidden, out_grad))


def weight_terms(pieces):
    row_tokens, gate_grad, up_grad, hidden, out_grad = pieces
    grad_gate = jnp.dot(row_tokens.T, gate_grad, preferred_element_type=jnp.float32)
    grad_up = jnp.dot(row_tokens.T, up_grad, preferred_element_type=jnp.float32)
    grad_down = jnp.dot(hidden.T, out_grad, preferred_element_type=jnp.float32)
    return (grad_gate, grad_up, grad_down)


def expert_pass(weight_gate, weight_up, weight_down, row_tokens, row_cotan, row_weights):
    row_grads, pieces = forward_rows(
        weight_gate, weight_up, weight_down, row_tokens, row_cotan, row_weights
    )
    return (row_grads, weight_terms(pieces))


def shards(tokens, cotangent, routes, combine, hot_experts, extra_slots, w_gate, w_up, w_down):
    expert_count = lax.axis_size("expert")
    token_count, features = tokens.shape
    route_count = routes.shape[1]
    capacity = max(2, min(token_count * route_count * 7 // (8 * expert_count), token_count // 2))
    spare_slots = 2 * max(1, capacity // 6)
    expert_ids = routes.reshape(-1)
    assign_count = expert_ids.shape[0]
    assign_order = jnp.arange(assign_count, dtype=jnp.int32)
    earlier = (expert_ids[:, None] == expert_ids[None, :]) & (
        assign_order[None, :] < assign_order[:, None]
    )
    slot_rank = jnp.sum(earlier.astype(jnp.int32), axis=1)
    hot_match = expert_ids[:, None] == hot_experts[None, :]
    slot_limit = capacity + jnp.sum(jnp.where(hot_match, extra_slots[None, :], 0), axis=1)
    is_kept = slot_rank < slot_limit
    slot_count = capacity + spare_slots
    total_slots = expert_count * slot_count
    flat_slot = jnp.where(is_kept, expert_ids * slot_count + slot_rank, total_slots)
    slot_ids = jnp.arange(total_slots, dtype=jnp.int32)
    assign_onehot = slot_ids[:, None] == flat_slot[None, :]
    token_onehot = jnp.any(
        assign_onehot.reshape(total_slots, token_count, route_count), axis=2
    ).astype(jnp.bfloat16)
    both_rows = jnp.concatenate([tokens, cotangent], axis=1)
    filled = jnp.dot(token_onehot, both_rows, preferred_element_type=jnp.float32).astype(
        jnp.bfloat16
    )
    token_send = filled[:, :features].reshape(expert_count, slot_count, features)
    cotan_send = filled[:, features:].reshape(expert_count, slot_count, features)
    weight_flat = jnp.sum(
        jnp.where(assign_onehot, combine.reshape(-1).astype(jnp.float32)[None, :], 0.0), axis=1
    )
    weight_send = weight_flat.astype(jnp.bfloat16).reshape(expert_count, slot_count)
    token_recv, cotan_recv, weight_recv = (
        lax.all_to_all(token_send, "expert", split_axis=0, concat_axis=0, tiled=True),
        lax.all_to_all(cotan_send, "expert", split_axis=0, concat_axis=0, tiled=True),
        lax.all_to_all(weight_send, "expert", split_axis=0, concat_axis=0, tiled=True),
    )
    own_weights = (w_gate[0], w_up[0], w_down[0])
    all_rows, grad_terms = expert_pass(
        own_weights[0],
        own_weights[1],
        own_weights[2],
        token_recv.reshape(-1, features),
        cotan_recv.reshape(-1, features),
        weight_recv.reshape(-1),
    )
    grad_rows = all_rows.reshape(expert_count, slot_count, features)
    returned_rows = lax.all_to_all(grad_rows, "expert", split_axis=0, concat_axis=0, tiled=True)
    token_grads = jnp.dot(
        token_onehot.T,
        returned_rows.reshape(total_slots, features),
        preferred_element_type=jnp.float32,
    ).astype(jnp.bfloat16)
    grad_gate, grad_up = (
        lax.psum_scatter(grad_terms[0][None], "dp", scatter_dimension=1, tiled=True),
        lax.psum_scatter(grad_terms[1][None], "dp", scatter_dimension=1, tiled=True),
    )
    grad_down = lax.psum(grad_terms[2][None], "dp")
    return (
        token_grads,
        grad_gate.astype(jnp.bfloat16),
        grad_up.astype(jnp.bfloat16),
        grad_down.astype(jnp.bfloat16),
    )


def solution(mesh):
    in_specs = (
        P(("dp", "expert"), None),
        P(("dp", "expert"), None),
        P(("dp", "expert"), None),
        P(("dp", "expert"), None),
        P(),
        P(),
        P("expert", None, None),
        P("expert", None, None),
        P("expert", None, None),
    )
    out_specs = (
        P(("dp", "expert"), None),
        P("expert", "dp", None),
        P("expert", "dp", None),
        P("expert", None, None),
    )
    return jax.shard_map(shards, mesh=mesh, in_specs=in_specs, out_specs=out_specs, check_vma=False)
```

profile of v0, /device:TPU:0, one launch (start us, length us, event | category | flops | bytes accessed | tf_op | source)
XLA Modules:
  0.0 155.9 jit_solution(16793875699837294183)
XLA Ops:
  7.2 0.8 copy.24
  8.3 0.8 copy.26
  9.1 0.8 select_reduce_fusion.1
  10.0 0.7 convert_element_type.116
  10.7 6.4 %all-to-all-start = ((bf16[8,1,20]{2,1,0:T(2,128)(2,1)}), bf16[8,1,20]{2,1,0:T(2,128)(2,1)S(1)}, u32[]{:S(2)}, u32[]{:S(2)}) async-start(bf16[8,1,20]{2,1,0:T(2,128)(2,1)} %convert_element_type.116), calls=%async_computation | async-start | bytes 8192 | tf_op jit(solution)/shard_map/all_to_all | solution.py:78
  17.4 1.2 convolution_convert_fusion
  18.7 0.8 reshape.99
  19.5 3.0 %all-to-all-done = bf16[8,1,20]{2,1,0:T(2,128)(2,1)S(1)} async-done(((bf16[8,1,20]{2,1,0:T(2,128)(2,1)}), bf16[8,1,20]{2,1,0:T(2,128)(2,1)S(1)}, u32[]{:S(2)}, u32[]{:S(2)}) %all-to-all-start) | async-done | bytes 352 | tf_op jit(solution)/shard_map/all_to_all | solution.py:78
  22.6 3.5 %all-to-all-start.2 = ((bf16[8,20,1024]{2,1,0:T(8,128)(2,1)}), bf16[8,20,1024]{2,1,0:T(8,128)(2,1)S(1)}, u32[]{:S(2)}, u32[]{:S(2)}) async-start(bf16[8,20,1024]{2,1,0:T(8,128)(2,1)} %reshape.99), calls=%async_computation.2 | async-start | bytes 786432 | tf_op jit(solution)/shard_map/all_to_all | solution.py:76
  26.1 0.8 reshape.98
  26.9 11.6 %all-to-all-done.2 = bf16[8,20,1024]{2,1,0:T(8,128)(2,1)S(1)} async-done(((bf16[8,20,1024]{2,1,0:T(8,128)(2,1)}), bf16[8,20,1024]{2,1,0:T(8,128)(2,1)S(1)}, u32[]{:S(2)}, u32[]{:S(2)}) %all-to-all-start.2) | async-done | bytes 327712 | tf_op jit(solution)/shard_map/all_to_all | solution.py:76
  38.5 3.5 %all-to-all-start.1 = ((bf16[8,20,1024]{2,1,0:T(8,128)(2,1)}), bf16[8,20,1024]{2,1,0:T(8,128)(2,1)S(1)}, u32[]{:S(2)}, u32[]{:S(2)}) async-start(bf16[8,20,1024]{2,1,0:T(8,128)(2,1)} %reshape.98), calls=%async_computation.1 | async-start | bytes 786432 | tf_op jit(solution)/shard_map/all_to_all | solution.py:77
  42.8 11.6 %all-to-all-done.1 = bf16[8,20,1024]{2,1,0:T(8,128)(2,1)S(1)} async-done(((bf16[8,20,1024]{2,1,0:T(8,128)(2,1)}), bf16[8,20,1024]{2,1,0:T(8,128)(2,1)S(1)}, u32[]{:S(2)}, u32[]{:S(2)}) %all-to-all-start.1) | async-done | bytes 327712 | tf_op jit(solution)/shard_map/all_to_all | solution.py:77
  54.6 1.6 multiply_convert_fusion.4
  56.2 1.6 %convolution_bitcast_fusion.2 = f32[1,1024,384]{2,1,0:T(8,128)} fusion(bf16[160,1024]{1,0:T(8,128)(2,1)S(1)} %reshape.100, bf16[160,384]{1,0:T(8,128)(2,1)S(1)} %get-tuple-element.7), kind=kOutput, calls=%fused_computation.3 | convolution fusion | flops 125829120 | bytes 2023424 | tf_op jit(solution)/shard_map/dot_general | solution.py:28
  57.9 1.6 %convolution_bitcast_fusion.1 = f32[1,1024,384]{2,1,0:T(8,128)} fusion(bf16[160,1024]{1,0:T(8,128)(2,1)S(1)} %reshape.100, bf16[160,384]{1,0:T(8,128)(2,1)S(1)} %get-tuple-element.6), kind=kOutput, calls=%fused_computation.2 | convolution fusion | flops 125829120 | bytes 2023424 | tf_op jit(solution)/shard_map/dot_general | solution.py:29
  59.6 0.4 fusion.1
  60.5 0.8 reshape.101
  61.3 3.5 %all-to-all-start.3 = ((bf16[8,20,1024]{2,1,0:T(8,128)(2,1)}), bf16[8,20,1024]{2,1,0:T(8,128)(2,1)S(1)}, u32[]{:S(2)}, u32[]{:S(2)}) async-start(bf16[8,20,1024]{2,1,0:T(8,128)(2,1)} %reshape.101), calls=%async_computation.3 | async-start | bytes 786432 | tf_op jit(solution)/shard_map/all_to_all | solution.py:90
  64.8 1.5 convolution_bitcast_fusion
  66.3 78.5 %all-reduce.1 = bf16[1,384,1024]{2,1,0:T(8,128)(2,1)} all-reduce(f32[1,384,1024]{2,1,0:T(8,128)S(1)} %convolution_bitcast_fusion), channel_id=1, replica_groups=mesh['dp'=4,'expert'=8] {'dp'}, use_global_device_ids=true, to_apply=%region_6.7 | all-reduce | flops 393216 | bytes 2359296 | tf_op jit(solution)/shard_map/psum | solution.py:100
  144.9 0.8 convolution_convert_fusion.1
  145.7 1.7 %convert_element_type.103 = bf16[1,256,384]{2,1,0:T(8,128)(2,1)} convert(f32[1,256,384]{2,1,0:T(8,128)} %reduce-scatter.3.cloned.1.call-done) | non-fusion elementwise | flops 98304 | bytes 589824 | tf_op jit(solution)/shard_map/convert_element_type | solution.py:103
  147.4 1.7 %convert_element_type.104 = bf16[1,256,384]{2,1,0:T(8,128)(2,1)} convert(f32[1,256,384]{2,1,0:T(8,128)} %reduce-scatter.5.cloned.1.call-done) | non-fusion elementwise | flops 98304 | bytes 589824 | tf_op jit(solution)/shard_map/convert_element_type | solution.py:104
  (36 shorter events, 2.6 us)
Async XLA Ops:
  7.2 34.9 %copy-start = (bf16[1,1024,384]{2,1,0:T(8,128)(2,1)S(1)}, bf16[1,1024,384]{2,1,0:T(8,128)(2,1)}, u32[]{:S(2)}) copy-start(bf16[1,1024,384]{2,1,0:T(8,128)(2,1)} %param.15) | copy-start | bytes 2359300
  10.7 11.9 %all-to-all-start = ((bf16[8,1,20]{2,1,0:T(2,128)(2,1)}), bf16[8,1,20]{2,1,0:T(2,128)(2,1)S(1)}, u32[]{:S(2)}, u32[]{:S(2)}) async-start(bf16[8,1,20]{2,1,0:T(2,128)(2,1)} %convert_element_type.116), calls=%async_computation | async-start | bytes 8192 | tf_op jit(solution)/shard_map/all_to_all | solution.py:78
  22.6 15.9 %all-to-all-start.2 = ((bf16[8,20,1024]{2,1,0:T(8,128)(2,1)}), bf16[8,20,1024]{2,1,0:T(8,128)(2,1)S(1)}, u32[]{:S(2)}, u32[]{:S(2)}) async-start(bf16[8,20,1024]{2,1,0:T(8,128)(2,1)} %reshape.99), calls=%async_computation.2 | async-start | bytes 786432 | tf_op jit(solution)/shard_map/all_to_all | solution.py:76
  26.9 15.6 %copy-start.1 = (bf16[1,1024,384]{2,1,0:T(8,128)(2,1)S(1)}, bf16[1,1024,384]{2,1,0:T(8,128)(2,1)}, u32[]{:S(2)}) copy-start(bf16[1,1024,384]{2,1,0:T(8,128)(2,1)} %param.16) | copy-start | bytes 2359300
  38.5 15.9 %all-to-all-start.1 = ((bf16[8,20,1024]{2,1,0:T(8,128)(2,1)}), bf16[8,20,1024]{2,1,0:T(8,128)(2,1)S(1)}, u32[]{:S(2)}, u32[]{:S(2)}) async-start(bf16[8,20,1024]{2,1,0:T(8,128)(2,1)} %reshape.98), calls=%async_computation.1 | async-start | bytes 786432 | tf_op jit(solution)/shard_map/all_to_all | solution.py:77
  42.0 103.7 %reduce-scatter.3.cloned.1.call-start = ((), (), s32[]{:S(2)}) async-start(), calls=%async_computation.6 | async-start | bytes 1966080 | tf_op jit(solution)/shard_map/reduce_scatter | solution.py:97
  42.5 17.1 %copy-start.2 = (f32[160,384]{1,0:T(8,128)}, f32[160,384]{1,0:T(8,128)S(1)}, u32[]{:S(2)}) copy-start(f32[160,384]{1,0:T(8,128)S(1)} %fusion.3) | copy-start | bytes 737284
  42.8 16.7 %copy-start.3 = (f32[160,384]{1,0:T(8,128)}, f32[160,384]{1,0:T(8,128)S(1)}, u32[]{:S(2)}) copy-start(f32[160,384]{1,0:T(8,128)S(1)} %fusion.6) | copy-start | bytes 737284
  57.8 89.6 %reduce-scatter.5.cloned.1.call-start = ((), (), s32[]{:S(2)}) async-start(), calls=%async_computation.7 | async-start | bytes 1966080 | tf_op jit(solution)/shard_map/reduce_scatter | solution.py:98
  61.3 83.5 %all-to-all-start.3 = ((bf16[8,20,1024]{2,1,0:T(8,128)(2,1)}), bf16[8,20,1024]{2,1,0:T(8,128)(2,1)S(1)}, u32[]{:S(2)}, u32[]{:S(2)}) async-start(bf16[8,20,1024]{2,1,0:T(8,128)(2,1)} %reshape.101), calls=%async_computation.3 | async-start | bytes 786432 | tf_op jit(solution)/shard_map/all_to_all | solution.py:90
Sparse Core Ops, SparseCore 0:
  57.9 36.4 reduce-scatter.2
  97.4 43.6 reduce-scatter.4
where the time goes:
time: 157 us; the launch traced here: 156 us
  blocking collectives  78.5 us (50%)
  waiting for transfers between devices  26.3 us (17%)
  starting transfers between devices  16.8 us (11%)
  between operations  14.2 us (9%)
  matrix products  9.84 us (6%)
  local copies, waits for them, and re-layouts  5.47 us (3%)
  other arithmetic  4.81 us (3%)
    psum x1, blocking collectives, shards(): grad_down = lax.psum(grad_terms[2][None], 'dp')  78.5 us
    all_to_all x1, waiting for transfers between devices, shards(): lax.all_to_all(token_send, 'expert', split_axis=0, concat_axis=0, tiled=T...  11.6 us
    all_to_all x1, waiting for transfers between devices, shards(): lax.all_to_all(cotan_send, 'expert', split_axis=0, concat_axis=0, tiled=T...  11.6 us
    all_to_all x1, starting transfers between devices, shards(): lax.all_to_all(weight_send, 'expert', split_axis=0, concat_axis=0, tiled=...  6.35 us
    all_to_all x1, starting transfers between devices, shards(): lax.all_to_all(grad_rows, 'expert', split_axis=0, concat_axis=0, tiled=True)  3.46 us
    all_to_all x1, starting transfers between devices, shards(): lax.all_to_all(token_send, 'expert', split_axis=0, concat_axis=0, tiled=T...  3.45 us
    all_to_all x1, starting transfers between devices, shards(): lax.all_to_all(cotan_send, 'expert', split_axis=0, concat_axis=0, tiled=T...  3.45 us
  transfers between devices with their start and end apart: 6, of which 3 were waited for; matrix products, arithmetic and copies ran while one was open for 7% of the time, Pallas kernels for 0%

commit v1 on v0

--- a/solution.py
+++ b/solution.py
@@ -97,7 +97,11 @@
         lax.psum_scatter(grad_terms[0][None], "dp", scatter_dimension=1, tiled=True),
         lax.psum_scatter(grad_terms[1][None], "dp", scatter_dimension=1, tiled=True),
     )
-    grad_down = lax.psum(grad_terms[2][None], "dp")
+    grad_down = grad_terms[2][None]
+    for hop in (1, 2):
+        grad_down = grad_down + lax.ppermute(
+            grad_down, "dp", [(dev, dev ^ hop) for dev in range(4)]
+        )
     return (
         token_grads,
         grad_gate.astype(jnp.bfloat16),

time: 157 us -> 170 us (1.083)
  waiting for transfers between devices: 26.3 us -> 96.4 us
  blocking collectives: 78.5 us -> 15.6 us
  other arithmetic: 4.81 us -> 10.8 us
    psum x1 -> x0, blocking collectives: 78.5 us -> none  [shards(): grad_down = lax.psum(grad_terms[2][None], 'dp')]
    ppermute x0 -> x2, waiting for transfers between devices: none -> 55.6 us  [shards(): lax.ppermute(grad_down, 'dp', [(dev, dev ^ hop) for dev in range(4)])]
    all_to_all x0 -> x1, blocking collectives: none -> 15.6 us  [shards(): lax.all_to_all(grad_rows, 'expert', split_axis=0, concat_axis=0, tiled=True)]
    reduce_scatter x1, waiting for transfers between devices: 0.01 us -> 13.9 us  [shards(): lax.psum_scatter(grad_terms[0][None], 'dp', scatter_dimension=1, tiled=True)]
    all_to_all x1 -> x0, starting transfers between devices: 3.46 us -> none  [shards(): lax.all_to_all(grad_rows, 'expert', split_axis=0, concat_axis=0, tiled=True)]
    add x0 -> x1, other arithmetic: none -> 3.06 us  [shards(): grad_down + lax.ppermute(grad_down, 'dp', [(dev, dev ^ hop) for dev in ra...]
    convert_element_type x0 -> x1, other arithmetic: none -> 2.98 us  [shards(): grad_down.astype(jnp.bfloat16)]
    ppermute x0 -> x2, starting transfers between devices: none -> 2.88 us  [shards(): lax.ppermute(grad_down, 'dp', [(dev, dev ^ hop) for dev in range(4)])]
  transfers between devices with their start and end apart: 6 -> 7, of which waited for: 3 -> 6; matrix products, arithmetic and copies ran while one was open for 7% -> 10% of each run, Pallas kernels for 0% -> 0%
where the time goes in v1:
time: 170 us; the launch traced here: 169 us
  waiting for transfers between devices  96.4 us (57%)
  starting transfers between devices  16.2 us (10%)
  blocking collectives  15.6 us (9%)
  between operations  14.2 us (8%)
  other arithmetic  10.8 us (6%)
  matrix products  9.63 us (6%)
  local copies, waits for them, and re-layouts  6.02 us (4%)
    ppermute x2, waiting for transfers between devices, shards(): lax.ppermute(grad_down, 'dp', [(dev, dev ^ hop) for dev in range(4)])  55.6 us
    all_to_all x1, blocking collectives, shards(): lax.all_to_all(grad_rows, 'expert', split_axis=0, concat_axis=0, tiled=True)  15.6 us
    reduce_scatter x1, waiting for transfers between devices, shards(): lax.psum_scatter(grad_terms[0][None], 'dp', scatter_dimension=1, tiled=True)  13.9 us
    all_to_all x1, waiting for transfers between devices, shards(): lax.all_to_all(token_send, 'expert', split_axis=0, concat_axis=0, tiled=T...  12.2 us
    all_to_all x1, waiting for transfers between devices, shards(): lax.all_to_all(cotan_send, 'expert', split_axis=0, concat_axis=0, tiled=T...  11.6 us
    all_to_all x1, starting transfers between devices, shards(): lax.all_to_all(weight_send, 'expert', split_axis=0, concat_axis=0, tiled=...  6.35 us
    all_to_all x1, starting transfers between devices, shards(): lax.all_to_all(token_send, 'expert', split_axis=0, concat_axis=0, tiled=T...  3.45 us
    all_to_all x1, starting transfers between devices, shards(): lax.all_to_all(cotan_send, 'expert', split_axis=0, concat_axis=0, tiled=T...  3.45 us
  transfers between devices with their start and end apart: 7, of which 6 were waited for; matrix products, arithmetic and copies ran while one was open for 10% of the time, Pallas kernels for 0%

profile of v1, /device:TPU:0, one launch (start us, length us, event | category | flops | bytes accessed | tf_op | source)
XLA Modules:
  0.0 168.9 jit_solution(3490447555295745100)
XLA Ops:
  7.2 0.8 copy.24
  10.7 6.4 %all-to-all-start = ((bf16[8,1,20]{2,1,0:T(2,128)(2,1)}), bf16[8,1,20]{2,1,0:T(2,128)(2,1)S(1)}, u32[]{:S(2)}, u32[]{:S(2)}) async-start(bf16[8,1,20]{2,1,0:T(2,128)(2,1)} %convert_element_type.116), calls=%async_computation | async-start | bytes 8192 | tf_op jit(solution)/shard_map/all_to_all | solution.py:78
  17.4 1.2 convolution_convert_fusion
  19.5 3.0 %all-to-all-done = bf16[8,1,20]{2,1,0:T(2,128)(2,1)S(1)} async-done(((bf16[8,1,20]{2,1,0:T(2,128)(2,1)}), bf16[8,1,20]{2,1,0:T(2,128)(2,1)S(1)}, u32[]{:S(2)}, u32[]{:S(2)}) %all-to-all-start) | async-done | bytes 352 | tf_op jit(solution)/shard_map/all_to_all | solution.py:78
  22.6 3.5 %all-to-all-start.1 = ((bf16[8,20,1024]{2,1,0:T(8,128)(2,1)}), bf16[8,20,1024]{2,1,0:T(8,128)(2,1)S(1)}, u32[]{:S(2)}, u32[]{:S(2)}) async-start(bf16[8,20,1024]{2,1,0:T(8,128)(2,1)} %reshape.98), calls=%async_computation.1 | async-start | bytes 786432 | tf_op jit(solution)/shard_map/all_to_all | solution.py:77
  26.0 0.8 reshape.99
  26.9 11.6 %all-to-all-done.1 = bf16[8,20,1024]{2,1,0:T(8,128)(2,1)S(1)} async-done(((bf16[8,20,1024]{2,1,0:T(8,128)(2,1)}), bf16[8,20,1024]{2,1,0:T(8,128)(2,1)S(1)}, u32[]{:S(2)}, u32[]{:S(2)}) %all-to-all-start.1) | async-done | bytes 327712 | tf_op jit(solution)/shard_map/all_to_all | solution.py:77
  38.5 3.5 %all-to-all-start.2 = ((bf16[8,20,1024]{2,1,0:T(8,128)(2,1)}), bf16[8,20,1024]{2,1,0:T(8,128)(2,1)S(1)}, u32[]{:S(2)}, u32[]{:S(2)}) async-start(bf16[8,20,1024]{2,1,0:T(8,128)(2,1)} %reshape.99), calls=%async_computation.2 | async-start | bytes 786432 | tf_op jit(solution)/shard_map/all_to_all | solution.py:76
  42.2 12.2 %all-to-all-done.2 = bf16[8,20,1024]{2,1,0:T(8,128)(2,1)S(1)} async-done(((bf16[8,20,1024]{2,1,0:T(8,128)(2,1)}), bf16[8,20,1024]{2,1,0:T(8,128)(2,1)S(1)}, u32[]{:S(2)}, u32[]{:S(2)}) %all-to-all-start.2) | async-done | bytes 327712 | tf_op jit(solution)/shard_map/all_to_all | solution.py:76
  55.6 1.1 multiply_convert_fusion.4
  56.7 1.6 convolution_bitcast_fusion.1
  58.5 0.9 reshape.106
  59.4 1.8 %convolution_bitcast_fusion = f32[1,384,1024]{2,1,0:T(8,128)S(1)} fusion(f32[160,1024]{1,0:T(8,128)} %reshape.106, f32[160]{0:T(256)S(1)} %reshape.105, f32[160,384]{1,0:T(8,128)} %copy-done.3, f32[160,384]{1,0:T(8,128)} %copy-done.2), kind=kOutput, calls=%fused_computation.2 | convolution fusion | flops 126525440 | bytes 2720384 | tf_op jit(solution)/shard_map/dot_general | solution.py:30
  61.2 1.6 collective-permute-start
  62.8 1.6 convolution_bitcast_fusion.2
  64.4 45.2 %collective-permute-done = f32[1,384,1024]{2,1,0:T(8,128)} collective-permute-done((f32[1,384,1024]{2,1,0:T(8,128)S(1)}, f32[1,384,1024]{2,1,0:T(8,128)}, u32[]{:S(2)}, u32[]{:S(2)}) %collective-permute-start) | collective-permute-done | bytes 1572896 | tf_op jit(solution)/shard_map/ppermute | solution.py:102
  109.6 3.1 %add.51 = f32[1,384,1024]{2,1,0:T(8,128)} add(f32[1,384,1024]{2,1,0:T(8,128)S(1)} %convolution_bitcast_fusion, f32[1,384,1024]{2,1,0:T(8,128)} %collective-permute-done) | non-fusion elementwise | flops 393216 | bytes 4718592 | tf_op jit(solution)/shard_map/add | solution.py:102
  112.7 1.3 collective-permute-start.1
  114.9 15.6 %all_to_all.21 = bf16[8,20,1024]{2,1,0:T(8,128)(2,1)S(1)} all-to-all(bf16[8,20,1024]{2,1,0:T(8,128)(2,1)S(1)} %reshape.101), channel_id=1, replica_groups=mesh['dp'=4,'expert'=8] {'expert'}, dimensions={0} | all-to-all | bytes 655360 | tf_op jit(solution)/shard_map/all_to_all | solution.py:90
  131.4 1.7 %convert_element_type.104 = bf16[1,256,384]{2,1,0:T(8,128)(2,1)} convert(f32[1,256,384]{2,1,0:T(8,128)} %reduce-scatter.5.cloned.1.call-done) | non-fusion elementwise | flops 98304 | bytes 589824 | tf_op jit(solution)/shard_map/convert_element_type | solution.py:108
  133.1 13.9 %reduce-scatter.3.cloned.1.call-done = f32[1,256,384]{2,1,0:T(8,128)} async-done(((f32[1,1024,384]{2,1,0:T(8,128)}), f32[1,256,384]{2,1,0:T(8,128)}) %reduce-scatter.3.cloned.1.call-update) | async-done | bytes 393232 | tf_op jit(solution)/shard_map/reduce_scatter | solution.py:97
  147.0 1.7 %convert_element_type.103 = bf16[1,256,384]{2,1,0:T(8,128)(2,1)} convert(f32[1,256,384]{2,1,0:T(8,128)} %reduce-scatter.3.cloned.1.call-done) | non-fusion elementwise | flops 98304 | bytes 589824 | tf_op jit(solution)/shard_map/convert_element_type | solution.py:107
  148.7 10.4 %collective-permute-done.1 = f32[1,384,1024]{2,1,0:T(8,128)} collective-permute-done((f32[1,384,1024]{2,1,0:T(8,128)}, f32[1,384,1024]{2,1,0:T(8,128)}, u32[]{:S(2)}, u32[]{:S(2)}) %collective-permute-start.1) | collective-permute-done | bytes 1572896 | tf_op jit(solution)/shard_map/ppermute | solution.py:102
  159.1 3.0 %add_convert_fusion = bf16[1,384,1024]{2,1,0:T(8,128)(2,1)} fusion(f32[1,384,1024]{2,1,0:T(8,128)} %add.51, f32[1,384,1024]{2,1,0:T(8,128)} %collective-permute-done.1), kind=kLoop, calls=%fused_computation.1 | loop fusion | flops 786432 | bytes 3932160 | tf_op jit(solution)/shard_map/convert_element_type | solution.py:109
  (50 shorter events, 7.3 us)
Async XLA Ops:
  7.2 47.3 %copy-start = (bf16[1,1024,384]{2,1,0:T(8,128)(2,1)S(1)}, bf16[1,1024,384]{2,1,0:T(8,128)(2,1)}, u32[]{:S(2)}) copy-start(bf16[1,1024,384]{2,1,0:T(8,128)(2,1)} %param.15) | copy-start | bytes 2359300
  10.7 11.9 %all-to-all-start = ((bf16[8,1,20]{2,1,0:T(2,128)(2,1)}), bf16[8,1,20]{2,1,0:T(2,128)(2,1)S(1)}, u32[]{:S(2)}, u32[]{:S(2)}) async-start(bf16[8,1,20]{2,1,0:T(2,128)(2,1)} %convert_element_type.116), calls=%async_computation | async-start | bytes 8192 | tf_op jit(solution)/shard_map/all_to_all | solution.py:78
  22.6 15.9 %all-to-all-start.1 = ((bf16[8,20,1024]{2,1,0:T(8,128)(2,1)}), bf16[8,20,1024]{2,1,0:T(8,128)(2,1)S(1)}, u32[]{:S(2)}, u32[]{:S(2)}) async-start(bf16[8,20,1024]{2,1,0:T(8,128)(2,1)} %reshape.98), calls=%async_computation.1 | async-start | bytes 786432 | tf_op jit(solution)/shard_map/all_to_all | solution.py:77
  38.5 15.9 %all-to-all-start.2 = ((bf16[8,20,1024]{2,1,0:T(8,128)(2,1)}), bf16[8,20,1024]{2,1,0:T(8,128)(2,1)S(1)}, u32[]{:S(2)}, u32[]{:S(2)}) async-start(bf16[8,20,1024]{2,1,0:T(8,128)(2,1)} %reshape.99), calls=%async_computation.2 | async-start | bytes 786432 | tf_op jit(solution)/shard_map/all_to_all | solution.py:76
  42.0 89.4 %reduce-scatter.5.cloned.1.call-start = ((), (), s32[]{:S(2)}) async-start(), calls=%async_computation.7 | async-start | bytes 1966080 | tf_op jit(solution)/shard_map/reduce_scatter | solution.py:98
  42.2 12.7 %copy-start.1 = (bf16[1,1024,384]{2,1,0:T(8,128)(2,1)S(1)}, bf16[1,1024,384]{2,1,0:T(8,128)(2,1)}, u32[]{:S(2)}) copy-start(bf16[1,1024,384]{2,1,0:T(8,128)(2,1)} %param.16) | copy-start | bytes 2359300
  54.5 1.1 copy-start.8
  54.8 3.7 %copy-start.2 = (f32[160,384]{1,0:T(8,128)}, f32[160,384]{1,0:T(8,128)S(1)}, u32[]{:S(2)}) copy-start(f32[160,384]{1,0:T(8,128)S(1)} %fusion.3) | copy-start | bytes 737284
  55.6 2.9 %copy-start.3 = (f32[160,384]{1,0:T(8,128)}, f32[160,384]{1,0:T(8,128)S(1)}, u32[]{:S(2)}) copy-start(f32[160,384]{1,0:T(8,128)S(1)} %fusion.6) | copy-start | bytes 737284
  56.7 1.7 copy-start.6
  58.4 88.7 %reduce-scatter.3.cloned.1.call-start = ((), (), s32[]{:S(2)}) async-start(), calls=%async_computation.6 | async-start | bytes 1966080 | tf_op jit(solution)/shard_map/reduce_scatter | solution.py:97
  59.4 3.4 %copy-start.4 = (bf16[160,384]{1,0:T(8,128)(2,1)S(1)}, bf16[160,384]{1,0:T(8,128)(2,1)}, u32[]{:S(2)}) copy-start(bf16[160,384]{1,0:T(8,128)(2,1)} %get-tuple-element.7) | copy-start | bytes 368644
  61.2 48.4 %collective-permute-start = (f32[1,384,1024]{2,1,0:T(8,128)S(1)}, f32[1,384,1024]{2,1,0:T(8,128)}, u32[]{:S(2)}, u32[]{:S(2)}) collective-permute-start(f32[1,384,1024]{2,1,0:T(8,128)S(1)} %convolution_bitcast_fusion), channel_id=1, source_target_pairs={{0,8},{8,0},{16,24},{24,16},{1,9},{9,1},{17,25},{25,17},{2,10},{10... | collective-permute-start | bytes 4718600 | tf_op jit(solution)/shard_map/ppermute | solution.py:102
  64.4 49.6 %copy-start.5 = (bf16[160,384]{1,0:T(8,128)(2,1)S(1)}, bf16[160,384]{1,0:T(8,128)(2,1)}, u32[]{:S(2)}) copy-start(bf16[160,384]{1,0:T(8,128)(2,1)} %get-tuple-element.7) | copy-start | bytes 368644
  112.7 1.7 %copy-start.7 = (bf16[160,384]{1,0:T(8,128)(2,1)S(1)}, bf16[160,384]{1,0:T(8,128)(2,1)}, u32[]{:S(2)}) copy-start(bf16[160,384]{1,0:T(8,128)(2,1)} %copy-done.6) | copy-start | bytes 368644
  112.7 46.4 %collective-permute-start.1 = (f32[1,384,1024]{2,1,0:T(8,128)}, f32[1,384,1024]{2,1,0:T(8,128)}, u32[]{:S(2)}, u32[]{:S(2)}) collective-permute-start(f32[1,384,1024]{2,1,0:T(8,128)} %add.51), channel_id=1, source_target_pairs={{0,16},{8,24},{16,0},{24,8},{1,17},{9,25},{17,1},{25,9},{2,18},{10... | collective-permute-start | bytes 4718600 | tf_op jit(solution)/shard_map/ppermute | solution.py:102
Sparse Core Ops, SparseCore 0:
  58.5 42.5 reduce-scatter.4
  104.1 42.9 reduce-scatter.2
